TPU v7x, 128 devices: a whole 4x4x4 slice. The times are simulated.
128 devices in a mesh: seq: 128 (over x, y, z, core).
Axes of the slice: x: 4, y: 4, z: 4, core: 2. Of those that a mesh axis runs over, the one named last changes fastest.
Arguments:
- inputs: bfloat16 [131072, 768], P('seq'), may hold values from -6 to 6
- weight_one: bfloat16 [768, 3, 768], P('seq'), may hold values from -0.125 to 0.125
- weight_two: bfloat16 [768, 3, 768], P('seq'), may hold values from -0.125 to 0.125
- cotangent: bfloat16 [131072, 768], P('seq'), may hold values from -6 to 6
Outputs:
- outputs: bfloat16 [131072, 768], P('seq')
- input_grad: bfloat16 [131072, 768], P('seq')
- grad_one: float32 [768, 3, 768], P('seq')
- grad_two: float32 [768, 3, 768], P('seq')
All inputs are finite; a program needn't handle non-finite values.
Results may differ from a plain program's by a relative error of at most 0.0056.
Values may be sent and summed in bfloat16 or wider, within the bound.
A program may use at most 128 MiB of HBM per device.

v0:
```python
import math

import jax
import jax.numpy as jnp
from jax import lax
from jax.sharding import PartitionSpec as P

DILATION_A = 32
DILATION_B = 64


def padded_2(block, sides, width):
    for axis, dim in sides:
        count = lax.axis_size(axis)
        forward = [(i, i + 1) for i in range(count - 1)]
        backward = [(target, source) for source, target in forward]
        low = lax.ppermute(
            lax.slice_in_dim(block, block.shape[dim] - width, None, axis=dim), axis, forward
        )
        high = lax.ppermute(lax.slice_in_dim(block, 0, width, axis=dim), axis, backward)
        block = jnp.concatenate([low, block, high], axis=dim)
    return block


def normalize(layer_in):
    residual_in = layer_in.astype(jnp.float32)
    inv_rms = lax.rsqrt(jnp.mean(residual_in * residual_in, axis=-1, keepdims=True) + 1e-06)
    normed = residual_in * inv_rms
    active = (0.5 * normed * (1.0 + jax.scipy.special.erf(normed * 0.7071067811865476))).astype(
        jnp.bfloat16
    )
    return (residual_in, normed, inv_rms, active)


def slope_of(normed):
    return (
        0.5 * (1.0 + jax.scipy.special.erf(normed * 0.7071067811865476))
        + normed * jnp.exp(-0.5 * normed * normed) * 0.3989422804014327
    )


def fetch_forward(shard):
    return lax.all_gather(shard, "seq", axis=0, tiled=True)


def fetch_backward(shard):
    return lax.all_gather(shard, "seq", axis=0, tiled=True)


def forward_layer(layer_in, weight, spacing):
    residual_in, normed, inv_rms, active = normalize(layer_in)
    padded = padded_2(active, (("seq", 0),), spacing)
    length = layer_in.shape[0]
    mixed = jnp.zeros((length, weight.shape[2]), jnp.float32)
    for tap in range(3):
        mixed = mixed + jnp.dot(
            padded[tap * spacing : tap * spacing + length],
            weight[:, tap, :],
            preferred_element_type=jnp.float32,
        )
    return ((residual_in + mixed).astype(jnp.bfloat16), padded, normed, inv_rms)


def weight_term(padded, grad_out, spacing, grad_scale):
    length = grad_out.shape[0]
    terms = []
    for tap in range(3):
        window = padded[tap * spacing : tap * spacing + length]
        terms.append(
            lax.dot_general(
                window, grad_out, (((0,), (0,)), ((), ())), preferred_element_type=jnp.float32
            )
        )
    return jnp.stack(terms, axis=1) * grad_scale


def reduce_layer(padded, grad_out, spacing, grad_scale):
    whole_term = weight_term(padded, grad_out, spacing, grad_scale)
    return lax.psum_scatter(whole_term, "seq", scatter_dimension=0, tiled=True)


def backward_layer(grad_out, normed, inv_rms, weight, spacing):
    length = grad_out.shape[0]
    grad_pad = padded_2(grad_out, (("seq", 0),), spacing)
    act_grad = jnp.zeros((length, weight.shape[0]), jnp.float32)
    for tap in range(3):
        start_row = (2 - tap) * spacing
        act_grad = act_grad + lax.dot_general(
            grad_pad[start_row : start_row + length],
            weight[:, tap, :],
            (((1,), (1,)), ((), ())),
            preferred_element_type=jnp.float32,
        )
    norm_grad = act_grad * slope_of(normed)
    passed = grad_out.astype(jnp.float32) + inv_rms * (
        norm_grad - normed * jnp.mean(norm_grad * normed, axis=-1, keepdims=True)
    )
    return passed.astype(jnp.bfloat16)


def per_device(inputs, weight_one, weight_two, cotangent):
    grad_scale = 1.0 / math.sqrt(inputs.shape[0] * lax.axis_size("seq"))
    full_one = fetch_forward(weight_one)
    hidden, pad_one, normed_one, inv_one = forward_layer(inputs, full_one, DILATION_A)
    full_two = fetch_forward(weight_two)
    outputs, pad_two, normed_two, inv_two = forward_layer(hidden, full_two, DILATION_B)
    back_two = fetch_backward(weight_two)
    hidden_grad = backward_layer(cotangent, normed_two, inv_two, back_two, DILATION_B)
    grad_two = reduce_layer(pad_two, cotangent, DILATION_B, grad_scale)
    back_one = fetch_backward(weight_one)
    input_grad = backward_layer(hidden_grad, normed_one, inv_one, back_one, DILATION_A)
    grad_one = reduce_layer(pad_one, hidden_grad, DILATION_A, grad_scale)
    return (outputs, input_grad, grad_one, grad_two)


def solution(mesh):
    in_specs = (P("seq", None), P("seq", None, None), P("seq", None, None), P("seq", None))
    out_specs = (P("seq", None), P("seq", None), P("seq", None, None), P("seq", None, None))
    return jax.shard_map(
        per_device, mesh=mesh, in_specs=in_specs, out_specs=out_specs, check_vma=False
    )
```

profile of v0, /device:TPU:1, one launch (start us, length us, event | category | flops | bytes accessed | tf_op | source)
XLA Modules:
  0.0 380.1 jit_solution(17278720018428972216)
XLA Ops:
  13.0 3.3 collective-permute-start.1
  16.4 3.5 collective-permute-start
  19.9 2.4 collective-permute-start.5
  24.3 57.8 %all-gather.3.cloned.1.call-done = bf16[768,3,768]{2,1,0:T(4,128)(2,1)} async-done(((bf16[6,3,768]{2,1,0:T(4,128)(2,1)}), bf16[768,3,768]{2,1,0:T(4,128)(2,1)}) %all-gather.3.cloned.1.call-update) | async-done | bytes 3538960 | tf_op jit(solution)/shard_map/all_gather | solution.py:43
  82.0 12.4 %fusion.69 = (bf16[768,1,768]{2,1,0:T(2,128)(2,1)}, bf16[768,1,768]{2,1,0:T(2,128)(2,1)S(1)}, bf16[768,1,768]{2,1,0:T(2,128)(2,1)}) fusion(bf16[768,3,768]{2,1,0:T(4,128)(2,1)} %all-gather.3.cloned.1.call-done), kind=kLoop, calls=%fused_computation.105 | loop fusion | bytes 7077888 | tf_op jit(solution)/shard_map/slice | solution.py:58
  95.8 3.1 fusion.53
  98.9 50.7 %all-gather.5.cloned.1.call-done = bf16[768,3,768]{2,1,0:T(4,128)(2,1)} async-done(((bf16[6,3,768]{2,1,0:T(4,128)(2,1)}), bf16[768,3,768]{2,1,0:T(4,128)(2,1)}) %all-gather.5.cloned.1.call-update) | async-done | bytes 3538960 | tf_op jit(solution)/shard_map/all_gather | solution.py:43
  149.6 11.4 %fusion.68 = (bf16[768,1,768]{2,1,0:T(2,128)(2,1)S(1)}, bf16[768,1,768]{2,1,0:T(2,128)(2,1)S(1)}, bf16[768,1,768]{2,1,0:T(2,128)(2,1)S(1)}) fusion(bf16[768,3,768]{2,1,0:T(4,128)(2,1)} %all-gather.5.cloned.1.call-done), kind=kLoop, calls=%fused_computation.104 | loop fusion | bytes 7077888 | tf_op jit(solution)/shard_map/slice | solution.py:58
  165.6 2.2 fusion.48
  167.8 2.5 fusion.46
  170.5 2.6 fusion.36
  173.1 2.6 fusion.35
  175.8 2.1 fusion.31
  181.4 2.4 collective-permute-start.3
  185.3 2.3 convolution_bitcast_fusion.3
  187.5 2.3 convolution_bitcast_fusion.5
  189.8 3.3 maximum_multiply_fusion
  196.1 3.2 maximum_multiply_fusion.1
  200.2 2.2 collective-permute-start.6
  202.4 3.1 fusion.55
  206.9 4.1 %collective-permute-start.7 = (bf16[32,768]{1,0:T(8,128)(2,1)S(1)}, bf16[32,768]{1,0:T(8,128)(2,1)S(1)}, u32[]{:S(2)}, u32[]{:S(2)}) collective-permute-start(bf16[32,768]{1,0:T(8,128)(2,1)S(1)} %get-tuple-element.26), channel_id=1, source_target_pairs={{0,1},{1,2},{2,3},{3,4},{4,5},{5,6},{6,7},{7,8},{8,9},{9,10},{10,1... | collective-permute-start | bytes 147464 | tf_op jit(solution)/shard_map/ppermute | solution.py:17
  212.5 2.6 fusion.21
  219.5 2.8 fusion.37
  222.3 148.9 %all-reduce.5.cloned.1.call-done = (f32[768,3,768]{2,0,1:T(8,128)}, f32[768,3,768]{2,0,1:T(8,128)}) async-done(((f32[768,3,768]{2,0,1:T(8,128)}, f32[768,3,768]{2,0,1:T(8,128)}), (f32[768,3,768]{2,0,1:T(8,128)}, f32[768,3,768]{2,0,1:T(8,128)})) %all-reduce.5.cloned.1.call-update) | async-done | bytes 14155792
  (82 shorter events, 32.0 us)
Async XLA Ops:
  7.2 3.5 copy-start
  7.2 74.8 %all-gather.3.cloned.1.call-start = ((), (), s32[]{:S(2)}) async-start(), calls=%async_computation | async-start | bytes 4755456 | tf_op jit(solution)/shard_map/all_gather | solution.py:43
  7.9 141.7 %all-gather.5.cloned.1.call-start = ((), (), s32[]{:S(2)}) async-start(), calls=%async_computation.1 | async-start | bytes 4755456 | tf_op jit(solution)/shard_map/all_gather | solution.py:43
  8.7 11.2 %copy-start.16 = (bf16[1024,768]{1,0:T(8,128)(2,1)S(1)}, bf16[1024,768]{1,0:T(8,128)(2,1)}, u32[]{:S(2)}) copy-start(bf16[1024,768]{1,0:T(8,128)(2,1)} %param.7) | copy-start | bytes 4718596
  8.7 362.6 %all-reduce.5.cloned.1.call-start = ((), (), s32[]{:S(2)}) async-start(), calls=%async_computation.2 | async-start | bytes 28311552
  13.0 157.3 %collective-permute-start.1 = (bf16[32,768]{1,0:T(8,128)(2,1)S(1)}, bf16[32,768]{1,0:T(8,128)(2,1)}, u32[]{:S(2)}, u32[]{:S(2)}) collective-permute-start(bf16[32,768]{1,0:T(8,128)(2,1)S(1)} %get-tuple-element.32), channel_id=1, source_target_pairs={{1,0},{2,1},{3,2},{4,3},{5,4},{6,5},{7,6},{8,7},{9,8},{10,9},{11,1... | collective-permute-start | bytes 147464 | tf_op jit(solution)/shard_map/ppermute | solution.py:20
  16.4 146.1 %collective-permute-start = (bf16[32,768]{1,0:T(8,128)(2,1)S(1)}, bf16[32,768]{1,0:T(8,128)(2,1)}, u32[]{:S(2)}, u32[]{:S(2)}) collective-permute-start(bf16[32,768]{1,0:T(8,128)(2,1)S(1)} %get-tuple-element.33), channel_id=1, source_target_pairs={{0,1},{1,2},{2,3},{3,4},{4,5},{5,6},{6,7},{7,8},{8,9},{9,10},{10,1... | collective-permute-start | bytes 147464 | tf_op jit(solution)/shard_map/ppermute | solution.py:17
  19.9 153.2 %collective-permute-start.5 = (bf16[64,768]{1,0:T(8,128)(2,1)S(1)}, bf16[64,768]{1,0:T(8,128)(2,1)S(1)}, u32[]{:S(2)}, u32[]{:S(2)}) collective-permute-start(bf16[64,768]{1,0:T(8,128)(2,1)S(1)} %get-tuple-element.28), channel_id=1, source_target_pairs={{0,1},{1,2},{2,3},{3,4},{4,5},{5,6},{6,7},{7,8},{8,9},{9,10},{10,1... | collective-permute-start | bytes 294920 | tf_op jit(solution)/shard_map/ppermute | solution.py:17
  22.3 145.5 %collective-permute-start.4 = (bf16[64,768]{1,0:T(8,128)(2,1)S(1)}, bf16[64,768]{1,0:T(8,128)(2,1)}, u32[]{:S(2)}, u32[]{:S(2)}) collective-permute-start(bf16[64,768]{1,0:T(8,128)(2,1)S(1)} %get-tuple-element.29), channel_id=1, source_target_pairs={{1,0},{2,1},{3,2},{4,3},{5,4},{6,5},{7,6},{8,7},{9,8},{10,9},{11,1... | collective-permute-start | bytes 294920 | tf_op jit(solution)/shard_map/ppermute | solution.py:20
  82.0 13.8 %copy-start.19 = (bf16[1024,768]{1,0:T(8,128)(2,1)S(1)}, bf16[1024,768]{1,0:T(8,128)(2,1)}, u32[]{:S(2)}) copy-start(bf16[1024,768]{1,0:T(8,128)(2,1)} %copy-done.18) | copy-start | bytes 4718596
  161.0 6.8 %copy-start.7 = (bf16[768,1,768]{2,1,0:T(2,128)(2,1)}, bf16[768,1,768]{2,1,0:T(2,128)(2,1)S(1)}, u32[]{:S(2)}) copy-start(bf16[768,1,768]{2,1,0:T(2,128)(2,1)S(1)} %get-tuple-element.20) | copy-start | bytes 3538948
  161.0 12.1 %copy-start.5 = (bf16[768,1,768]{2,1,0:T(2,128)(2,1)}, bf16[768,1,768]{2,1,0:T(2,128)(2,1)S(1)}, u32[]{:S(2)}) copy-start(bf16[768,1,768]{2,1,0:T(2,128)(2,1)S(1)} %get-tuple-element.18) | copy-start | bytes 3538948
  161.0 3.4 copy-start.11
  161.0 4.6 %copy-start.20 = (bf16[1024,768]{1,0:T(8,128)(2,1)S(1)}, bf16[1024,768]{1,0:T(8,128)(2,1)}, u32[]{:S(2)}) copy-start(bf16[1024,768]{1,0:T(8,128)(2,1)} %copy-done.18) | copy-start | bytes 4718596
  173.1 2.7 copy-start.3
  177.9 9.6 %copy-start.1 = (bf16[1024,768]{1,0:T(8,128)(2,1)}, bf16[1024,768]{1,0:T(8,128)(2,1)S(1)}, u32[]{:S(2)}) copy-start(bf16[1024,768]{1,0:T(8,128)(2,1)S(1)} %get-tuple-element.24) | copy-start | bytes 4718596
  179.4 15.1 %collective-permute-start.2 = (bf16[64,768]{1,0:T(8,128)(2,1)S(1)}, bf16[64,768]{1,0:T(8,128)(2,1)S(1)}, u32[]{:S(2)}, u32[]{:S(2)}) collective-permute-start(bf16[64,768]{1,0:T(8,128)(2,1)S(1)} %get-tuple-element.31), channel_id=1, source_target_pairs={{0,1},{1,2},{2,3},{3,4},{4,5},{5,6},{6,7},{7,8},{8,9},{9,10},{10,1... | collective-permute-start | bytes 294920 | tf_op jit(solution)/shard_map/ppermute | solution.py:17
  181.4 11.7 %collective-permute-start.3 = (bf16[64,768]{1,0:T(8,128)(2,1)S(1)}, bf16[64,768]{1,0:T(8,128)(2,1)S(1)}, u32[]{:S(2)}, u32[]{:S(2)}) collective-permute-start(bf16[64,768]{1,0:T(8,128)(2,1)S(1)} %get-tuple-element.30), channel_id=1, source_target_pairs={{1,0},{2,1},{3,2},{4,3},{5,4},{6,5},{7,6},{8,7},{9,8},{10,9},{11,1... | collective-permute-start | bytes 294920 | tf_op jit(solution)/shard_map/ppermute | solution.py:20
  200.2 5.3 %copy-start.2 = (bf16[1024,768]{1,0:T(8,128)(2,1)S(1)}, bf16[1024,768]{1,0:T(8,128)(2,1)}, u32[]{:S(2)}) copy-start(bf16[1024,768]{1,0:T(8,128)(2,1)} %copy-done.1) | copy-start | bytes 4718596
  200.2 5.3 %copy-start.14 = (bf16[768,1,768]{2,1,0:T(2,128)(2,1)S(1)}, bf16[768,1,768]{2,1,0:T(2,128)(2,1)}, u32[]{:S(2)}) copy-start(bf16[768,1,768]{2,1,0:T(2,128)(2,1)} %copy-done.13) | copy-start | bytes 3538948
  200.2 10.9 %collective-permute-start.6 = (bf16[32,768]{1,0:T(8,128)(2,1)S(1)}, bf16[32,768]{1,0:T(8,128)(2,1)S(1)}, u32[]{:S(2)}, u32[]{:S(2)}) collective-permute-start(bf16[32,768]{1,0:T(8,128)(2,1)S(1)} %get-tuple-element.27), channel_id=1, source_target_pairs={{1,0},{2,1},{3,2},{4,3},{5,4},{6,5},{7,6},{8,7},{9,8},{10,9},{11,1... | collective-permute-start | bytes 147464 | tf_op jit(solution)/shard_map/ppermute | solution.py:20
  205.4 5.6 %copy-start.12 = (bf16[768,1,768]{2,1,0:T(2,128)(2,1)S(1)}, bf16[768,1,768]{2,1,0:T(2,128)(2,1)}, u32[]{:S(2)}) copy-start(bf16[768,1,768]{2,1,0:T(2,128)(2,1)} %get-tuple-element.23) | copy-start | bytes 3538948
  206.9 5.6 %copy-start.10 = (bf16[768,1,768]{2,1,0:T(2,128)(2,1)S(1)}, bf16[768,1,768]{2,1,0:T(2,128)(2,1)}, u32[]{:S(2)}) copy-start(bf16[768,1,768]{2,1,0:T(2,128)(2,1)} %get-tuple-element.21) | copy-start | bytes 3538948
  206.9 5.6 %collective-permute-start.7 = (bf16[32,768]{1,0:T(8,128)(2,1)S(1)}, bf16[32,768]{1,0:T(8,128)(2,1)S(1)}, u32[]{:S(2)}, u32[]{:S(2)}) collective-permute-start(bf16[32,768]{1,0:T(8,128)(2,1)S(1)} %get-tuple-element.26), channel_id=1, source_target_pairs={{0,1},{1,2},{2,3},{3,4},{4,5},{5,6},{6,7},{7,8},{8,9},{9,10},{10,1... | collective-permute-start | bytes 147464 | tf_op jit(solution)/shard_map/ppermute | solution.py:17
  (9 other events, 17.7 us)
Sparse Core Ops, SparseCore 0:
  11.0 70.9 all-gather.2
  85.0 64.5 all-gather.4
  199.4 171.7 all-reduce.4
where the time goes:
time: 381 us; the launch traced here: 380 us
  waiting for transfers between devices  259 us (68%)
  matrix products  37.6 us (10%)
  local copies, waits for them, and re-layouts  33.7 us (9%)
  starting transfers between devices  21.9 us (6%)
  between operations  14.3 us (4%)
  other arithmetic  13.8 us (4%)
    unnamed x4, waiting for transfers between devices  150 us
    all_gather x2, waiting for transfers between devices, fetch_forward(): return lax.all_gather(shard, 'seq', axis=0, tiled=True)  109 us
    slice x2, local copies, waits for them, and re-layouts, forward_layer(): weight[:, tap, :]  23.7 us
    dot_general x6, matrix products, forward_layer(): jnp.dot(padded[tap * spacing:tap * spacing + length], weight[:, tap, :],...  15.1 us
    dot_general x6, matrix products, backward_layer(): lax.dot_general(grad_pad[start_row:start_row + length], weight[:, tap, :]...  12 us
    ppermute x4, starting transfers between devices, padded_2(): lax.ppermute(lax.slice_in_dim(block, block.shape[dim] - width, None, axis...  12 us
    dot_general x6, matrix products, weight_term(): lax.dot_general(window, grad_out, (((0,), (0,)), ((), ())), preferred_ele...  10.4 us
    ppermute x4, starting transfers between devices, padded_2(): lax.ppermute(lax.slice_in_dim(block, 0, width, axis=dim), axis, backward)  9.84 us
  transfers between devices with their start and end apart: 11, of which 3 were waited for; matrix products, arithmetic and copies ran while one was open for 17% of the time, Pallas kernels for 0%

commit v1 on v0

v1 whole, which is shorter than its diff:
```python
import math

import jax
import jax.numpy as jnp
from jax import lax
from jax.experimental import pallas as pl
from jax.experimental.pallas import tpu as pltpu
from jax.sharding import PartitionSpec as P

DILATION_A = 32
DILATION_B = 64
N = 128
C = 768
HALF = C // 2
L = 1024
BF = jnp.bfloat16
F32 = jnp.float32
MESH = pl.DeviceIdType.MESH
TM = 256


def body(
    scale,
    x_hbm, g_hbm, w_hbm,
    out_hbm, ig_hbm, gr_hbm,
    xb, a1p, h, a2p, g2p, g1p, at1, at2, W, s1, s2, ir1, ir2, G, stage, R0, A, H1, R1, B, S2R, T, S3S, S3R, ob, ib, gout,
    lsem, cs, cr, hs, hr, p1s, p1r, p2s, p2r, fs, fr, bs, br,
    x0s, x0r, x1s, x1r, x2s, x2r, x3s, x3r, x4s, x4r,
):
    me = lax.axis_index("seq")
    c = lax.rem(me, 2)
    z = lax.rem(me // 2, 4)
    y = lax.rem(me // 8, 4)
    x = me // 32
    g = me // 8

    def block(df, ds, o):
        xx = lax.rem(x + 4 + df * (1 - o) + ds * o, 4)
        yy = lax.rem(y + 4 + df * o + ds * (1 - o), 4)
        return 4 * xx + yy

    def dev(df, ds):
        return block(df, ds, c) * 8 + 2 * z + c

    sibling = me + 1 - 2 * c
    left = lax.rem(me + N - 1, N)
    right = lax.rem(me + 1, N)
    column = g * 8
    myf = x * (1 - c) + y * c
    mys = y * (1 - c) + x * c

    def remote(src, dst, send, recv, target):
        return pltpu.make_async_remote_copy(
            src_ref=src, dst_ref=dst, send_sem=send, recv_sem=recv, device_id=(target,), device_id_type=MESH
        )

    sent = []

    def send(*args):
        copy = remote(*args)
        copy.start()
        sent.append(copy)

    def arrived(dst, send_sem, recv_sem):
        remote(dst, dst, send_sem, recv_sem, sibling).wait_recv()

    load_x = pltpu.make_async_copy(x_hbm, xb, lsem.at[0])
    load_x.start()
    load_g = pltpu.make_async_copy(g_hbm, g2p.at[pl.ds(DILATION_B, L)], lsem.at[1])
    load_g.start()

    barrier = pltpu.get_barrier_semaphore()
    greet = []
    for k in range(1, 8):
        greet.append(column + lax.rem(me - column + k, 8))
    for k in range(1, 4):
        greet.append(dev(k, 0))
    greet += [dev(0, 1), dev(0, 3), left, right]
    for target in greet:
        pl.semaphore_signal(barrier, inc=1, device_id=(target,), device_id_type=MESH)
    pl.semaphore_wait(barrier, len(greet))

    cc = z // 2
    slot = 2 * lax.rem(z, 2) + c

    def column_send(l):
        for zt in range(4):
            target = column + 2 * zt + cc

            @pl.when(target != me)
            def _():
                remote(w_hbm.at[l], stage.at[l, :, slot], cs.at[l, zt], cr.at[l, slot], target).start()

            @pl.when(target == me)
            def _():
                pltpu.make_async_copy(w_hbm.at[l], stage.at[l, :, slot], cr.at[l, slot]).start()

    def column_wait(l):
        for j in range(4):
            source = column + 4 * c + j

            @pl.when(source != me)
            def _():
                arrived(stage.at[l, :, j], cs.at[l, 0], cr.at[l, j])

            @pl.when(source == me)
            def _():
                pltpu.make_async_copy(w_hbm.at[l], stage.at[l, :, j], cr.at[l, j]).wait()

    def column_sent(l):
        for zt in range(4):
            target = column + 2 * zt + cc

            @pl.when(target != me)
            def _():
                remote(w_hbm.at[l], stage.at[l, :, slot], cs.at[l, zt], cr.at[l, slot], target).wait_send()

    def blk(l, b, half):
        return W.at[l, :, b, half]

    def repack(l):
        row = lax.broadcasted_iota(jnp.int32, (24, 32), 0)
        col = lax.broadcasted_iota(jnp.int32, (24, 32), 1)
        pick = jnp.where(col == (row // 6) * 8 + lax.rem(row, 6), 1.0, 0.0).astype(BF)
        for k in range(3):
            dense = jnp.dot(pick, stage[l, k].reshape(32, C), preferred_element_type=F32)
            W[l, k, g, c] = dense.astype(BF)

    def ag_p1(l):
        for k in range(1, 4):
            send(blk(l, g, c), blk(l, g, c), p1s.at[l, k - 1], p1r.at[l, k - 1], dev(k, 0))

    def to_sibling(l, n, b):
        send(blk(l, b, c), blk(l, b, c), bs.at[l, n], br.at[l, n], sibling)

    def ag_p2(l, i):
        b = block(-i, 0, c)
        for d in range(2):
            send(blk(l, b, c), blk(l, b, c), p2s.at[l, d, i], p2r.at[l, d, i], dev(0, 1 + 2 * d))
        to_sibling(l, i, b)

    def ag_mid(l):
        for k in range(1, 4):
            arrived(blk(l, block(-k, 0, c), c), p1s.at[l, k - 1], p1r.at[l, k - 1])
            ag_p2(l, k)

    def ag_forward(l):
        for i in range(4):
            for d in range(2):
                b = block(-i, 3 - 2 * d, c)
                arrived(blk(l, b, c), p2s.at[l, d, i], p2r.at[l, d, i])
                part = W.at[l, :, b, c, :, pl.ds(HALF * d, HALF)]
                send(part, part, fs.at[l, d, i], fr.at[l, d, i], dev(0, 1 + 2 * d))
                to_sibling(l, 4 + 4 * d + i, b)

    def ag_last(l):
        for i in range(4):
            b = block(-i, 2, c)
            for d in range(2):
                part = W.at[l, :, b, c, :, pl.ds(HALF * d, HALF)]
                arrived(part, fs.at[l, d, i], fr.at[l, d, i])
            to_sibling(l, 12 + i, b)

    def ag_done(l):
        for n, ds in enumerate((0, 3, 1, 2)):
            for i in range(4):
                b = block(-i, ds, 1 - c)
                arrived(blk(l, b, 1 - c), bs.at[l, 4 * n + i], br.at[l, 4 * n + i])

    def halo_send(ref, d, n):
        send(ref.at[pl.ds(L, d)], ref.at[pl.ds(0, d)], hs.at[n, 0], hr.at[n, 0], right)
        send(ref.at[pl.ds(d, d)], ref.at[pl.ds(L + d, d)], hs.at[n, 1], hr.at[n, 1], left)

    def halo_wait(ref, d, n):
        arrived(ref.at[pl.ds(0, d)], hs.at[n, 0], hr.at[n, 0])
        arrived(ref.at[pl.ds(L + d, d)], hs.at[n, 1], hr.at[n, 1])

        @pl.when(me == 0)
        def _():
            ref[pl.ds(0, d), :] = jnp.zeros((d, C), BF)

        @pl.when(me == N - 1)
        def _():
            ref[pl.ds(L + d, d), :] = jnp.zeros((d, C), BF)

    def activate(xf, t0, ap, d, at, s_ref, ir_ref):
        inv = lax.rsqrt(jnp.mean(xf * xf, axis=-1, keepdims=True) + 1e-06)
        normed = xf * inv
        gate = 0.5 * (1.0 + lax.erf(normed * 0.7071067811865476))
        active = (normed * gate).astype(BF)
        ap[pl.ds(pl.multiple_of(t0 + d, 32), TM), :] = active
        at[:, pl.ds(t0, TM)] = active.T
        s_ref[pl.ds(t0, TM), :] = gate + normed * jnp.exp(-0.5 * normed * normed) * 0.3989422804014327
        ir_ref[pl.ds(t0, TM), :] = inv

    def tiles(fn, count=L // TM, size=TM):
        def step(i, carry):
            fn(pl.multiple_of(i * size, size))
            return carry

        lax.fori_loop(0, count, step, 0)

    def weight(l, k):
        return W[l, k].reshape(C, C)

    def forward(ap, d, l, t0):
        acc = jnp.zeros((TM, C), F32)
        for k in range(3):
            acc = acc + jnp.dot(
                ap[pl.ds(pl.multiple_of(t0 + k * d, 32), TM), :], weight(l, k), preferred_element_type=F32
            )
        return acc

    def backward(gp, d, l, x_ref, s_ref, ir_ref, t0):
        acc = jnp.zeros((TM, C), F32)
        for k in range(3):
            acc = acc + lax.dot_general(
                gp[pl.ds(pl.multiple_of(t0 + (2 - k) * d, 32), TM), :],
                weight(l, k),
                (((1,), (1,)), ((), ())),
                preferred_element_type=F32,
            )
        rows = pl.ds(t0, TM)
        inv = ir_ref[rows, :]
        normed = x_ref[rows, :].astype(F32) * inv
        norm_grad = acc * s_ref[rows, :]
        mean = jnp.mean(norm_grad * normed, axis=-1, keepdims=True)
        own = gp[pl.ds(pl.multiple_of(t0 + d, 32), TM), :].astype(F32)
        return (own + inv * (norm_grad - normed * mean)).astype(BF)

    def weight_grad(at, gp, d, l, k):
        rhs_start = (2 - k) * d

        def one(t0):
            acc = jnp.dot(at[pl.ds(t0, 384), :], gp[pl.ds(rhs_start, L), :], preferred_element_type=F32)
            b0 = t0 // 48
            G[l, k, pl.ds(b0, 8)] = acc.astype(BF).reshape(8, 2, 24, C)

        tiles(one, 2, 384)
        send(G.at[l, k, :, 1 - c], R0.at[l, k], x0s.at[l, k], x0r.at[l, k], sibling)

    def rs1(l, k):
        arrived(R0.at[l, k], x0s.at[l, k], x0r.at[l, k])

        def add(b, carry):
            s = b // 4
            f = lax.rem(b, 4)
            gb = f * (4 - 3 * c) + s * (1 + 3 * c)
            A[l, k, s, f] = (G[l, k, gb, c].astype(F32) + R0[l, k, gb].astype(F32)).astype(BF)
            return carry

        lax.fori_loop(0, 16, add, 0)
        far = lax.rem(mys + 2, 4)
        for d in range(2):
            send(
                A.at[l, k, far, :, :, pl.ds(HALF * d, HALF)], H1.at[l, k, d],
                x1s.at[l, k, d], x1r.at[l, k, d], dev(0, 1 + 2 * d),
            )

    def rs2(l, k):
        for d in range(2):
            arrived(H1.at[l, k, d], x1s.at[l, k, d], x1r.at[l, k, d])
            near = lax.rem(mys + 1 + 2 * d, 4)
            cols = pl.ds(HALF * d, HALF)
            A[l, k, near, :, :, cols] = (A[l, k, near, :, :, cols].astype(F32) + H1[l, k, d].astype(F32)).astype(BF)
            send(A.at[l, k, near], R1.at[l, k, d], x2s.at[l, k, d], x2r.at[l, k, d], dev(0, 1 + 2 * d))

    def rs3(l, k):
        for d in range(2):
            arrived(R1.at[l, k, d], x2s.at[l, k, d], x2r.at[l, k, d])
        B[l, k] = (A[l, k, mys].astype(F32) + R1[l, k, 0].astype(F32) + R1[l, k, 1].astype(F32)).astype(BF)
        for d in range(1, 4):
            send(
                B.at[l, k, lax.rem(myf + d, 4)], S2R.at[l, k, d - 1],
                x3s.at[l, k, d - 1], x3r.at[l, k, d - 1], dev(d, 0),
            )

    def rs4(l, k):
        for d in range(1, 4):
            arrived(S2R.at[l, k, d - 1], x3s.at[l, k, d - 1], x3r.at[l, k, d - 1])
        total = B[l, k, myf].astype(F32)
        for d in range(3):
            total = total + S2R[l, k, d].astype(F32)
        T[pl.ds(0, 24), :] = total
        T[pl.ds(24, 8), :] = jnp.zeros((8, C), F32)
        for j in range(4):
            S3S[l, j, k] = T[pl.ds(6 * j, 8), :].astype(BF)

    def rs5(l):
        for j in range(4):
            target = column + 4 * c + j

            @pl.when(target != me)
            def _():
                remote(S3S.at[l, j], S3R.at[l, z], x4s.at[l, j], x4r.at[l, z], target).start()

            @pl.when(target == me)
            def _():
                S3R[l, z] = S3S[l, j]

    def rs6(l):
        for zs in range(4):
            source = column + 2 * zs + cc

            @pl.when(source != me)
            def _():
                arrived(S3R.at[l, zs], x4s.at[l, 0], x4r.at[l, zs])

        total = S3R[l, 0].astype(F32)
        for zs in range(1, 4):
            total = total + S3R[l, zs].astype(F32)
        gout[l] = total * scale
        pltpu.make_async_copy(gout.at[l], gr_hbm.at[l], lsem.at[2 + l]).start()

    def rs_sent(l):
        for j in range(4):
            target = column + 4 * c + j

            @pl.when(target != me)
            def _():
                remote(S3S.at[l, j], S3R.at[l, z], x4s.at[l, j], x4r.at[l, z], target).wait_send()

    column_send(0)
    column_send(1)
    load_x.wait()
    tiles(lambda t0: activate(xb[pl.ds(t0, TM), :].astype(F32), t0, a1p, DILATION_A, at1, s1, ir1))
    column_wait(0)
    repack(0)
    ag_p1(0)
    ag_p2(0, 0)
    halo_send(a1p, DILATION_A, 0)
    ag_mid(0)
    column_wait(1)
    repack(1)
    ag_p1(1)
    load_g.wait()
    halo_send(g2p, DILATION_B, 2)
    ag_forward(0)
    ag_p2(1, 0)
    ag_mid(1)
    ag_last(0)
    halo_wait(a1p, DILATION_A, 0)
    ag_done(0)

    def first(t0):
        mixed = forward(a1p, DILATION_A, 0, t0)
        out = (xb[pl.ds(t0, TM), :].astype(F32) + mixed).astype(BF)
        h[pl.ds(t0, TM), :] = out
        activate(out.astype(F32), t0, a2p, DILATION_B, at2, s2, ir2)

    tiles(first)
    halo_send(a2p, DILATION_B, 1)
    ag_forward(1)
    halo_wait(g2p, DILATION_B, 2)
    weight_grad(at2, g2p, DILATION_B, 1, 0)
    ag_last(1)
    weight_grad(at2, g2p, DILATION_B, 1, 1)
    rs1(1, 0)
    weight_grad(at2, g2p, DILATION_B, 1, 2)
    rs1(1, 1)
    rs2(1, 0)
    ag_done(1)

    def second(t0):
        passed = backward(g2p, DILATION_B, 1, h, s2, ir2, t0)
        g1p[pl.ds(pl.multiple_of(t0 + DILATION_A, 32), TM), :] = passed

    tiles(second)
    halo_send(g1p, DILATION_A, 3)
    rs1(1, 2)
    rs2(1, 1)
    rs3(1, 0)
    weight_grad(at1, g1p, DILATION_A, 0, 1)
    halo_wait(g1p, DILATION_A, 3)
    rs2(1, 2)
    rs3(1, 1)
    rs4(1, 0)
    weight_grad(at1, g1p, DILATION_A, 0, 0)
    rs1(0, 1)
    rs3(1, 2)
    rs4(1, 1)
    weight_grad(at1, g1p, DILATION_A, 0, 2)
    rs1(0, 0)
    rs2(0, 1)
    rs4(1, 2)
    rs5(1)
    halo_wait(a2p, DILATION_B, 1)

    def last_forward(t0):
        mixed = forward(a2p, DILATION_B, 1, t0)
        rows = pl.ds(t0, TM)
        ob[rows, :] = (h[rows, :].astype(F32) + mixed).astype(BF)

    tiles(last_forward)
    store_out = pltpu.make_async_copy(ob, out_hbm, lsem.at[4])
    store_out.start()
    rs1(0, 2)
    rs2(0, 0)
    rs3(0, 1)
    rs6(1)

    def last_backward(t0):
        ib[pl.ds(t0, TM), :] = backward(g1p, DILATION_A, 0, xb, s1, ir1, t0)

    tiles(last_backward)
    store_in = pltpu.make_async_copy(ib, ig_hbm, lsem.at[5])
    store_in.start()
    rs2(0, 2)
    rs3(0, 0)
    rs4(0, 1)
    rs3(0, 2)
    rs4(0, 0)
    rs4(0, 2)
    rs5(0)
    rs6(0)

    for copy in sent:
        copy.wait_send()
    for l in range(2):
        column_sent(l)
        rs_sent(l)
        pltpu.make_async_copy(gout.at[l], gr_hbm.at[l], lsem.at[2 + l]).wait()
    store_out.wait()
    store_in.wait()


def per_device(inputs, weight_one, weight_two, cotangent):
    scale = 1.0 / math.sqrt(inputs.shape[0] * lax.axis_size("seq"))
    shards = jnp.stack([weight_one, weight_two]).transpose(0, 2, 1, 3)
    shards = jnp.pad(shards, ((0, 0), (0, 0), (0, 2), (0, 0)))
    anywhere = pl.BlockSpec(memory_space=pl.ANY)
    vmem = pltpu.VMEM
    dma = pltpu.SemaphoreType.DMA

    def kernel(*refs):
        body(scale, *refs)

    outputs, input_grad, grads = pl.pallas_call(
        kernel,
        out_shape=(
            jax.ShapeDtypeStruct((L, C), BF),
            jax.ShapeDtypeStruct((L, C), BF),
            jax.ShapeDtypeStruct((2, 3, 8, C), F32),
        ),
        in_specs=[anywhere] * 3,
        out_specs=(anywhere,) * 3,
        scratch_shapes=[
            vmem((L, C), BF),
            vmem((L + 2 * DILATION_A, C), BF),
            vmem((L, C), BF),
            vmem((L + 2 * DILATION_B, C), BF),
            vmem((L + 2 * DILATION_B, C), BF),
            vmem((L + 2 * DILATION_A, C), BF),
            vmem((C, L), BF),
            vmem((C, L), BF),
            vmem((2, 3, 16, 2, 24, C), BF),
            vmem((L, C), F32),
            vmem((L, C), F32),
            vmem((L, 1), F32),
            vmem((L, 1), F32),
            vmem((2, 3, 16, 2, 24, C), BF),
            vmem((2, 3, 4, 8, C), BF),
            vmem((2, 3, 16, 24, C), BF),
            vmem((2, 3, 4, 4, 24, C), BF),
            vmem((2, 3, 2, 4, 24, HALF), BF),
            vmem((2, 3, 2, 4, 24, C), BF),
            vmem((2, 3, 4, 24, C), BF),
            vmem((2, 3, 3, 24, C), BF),
            vmem((32, C), F32),
            vmem((2, 4, 3, 8, C), BF),
            vmem((2, 4, 3, 8, C), BF),
            vmem((L, C), BF),
            vmem((L, C), BF),
            vmem((2, 3, 8, C), F32),
            dma((6,)),
            dma((2, 4)), dma((2, 4)),
            dma((4, 2)), dma((4, 2)),
            dma((2, 3)), dma((2, 3)),
            dma((2, 2, 4)), dma((2, 2, 4)),
            dma((2, 2, 4)), dma((2, 2, 4)),
            dma((2, 16)), dma((2, 16)),
            dma((2, 3)), dma((2, 3)),
            dma((2, 3, 2)), dma((2, 3, 2)),
            dma((2, 3, 2)), dma((2, 3, 2)),
            dma((2, 3, 3)), dma((2, 3, 3)),
            dma((2, 4)), dma((2, 4)),
        ],
        compiler_params=pltpu.CompilerParams(
            collective_id=0, has_side_effects=True, vmem_limit_bytes=64000000
        ),
    )(inputs, cotangent, shards)
    grads = grads[:, :, :6, :].transpose(0, 2, 1, 3)
    return (outputs, input_grad, grads[0], grads[1])


def solution(mesh):
    in_specs = (P("seq", None), P("seq", None, None), P("seq", None, None), P("seq", None))
    out_specs = (P("seq", None), P("seq", None), P("seq", None, None), P("seq", None, None))
    return jax.shard_map(
        per_device, mesh=mesh, in_specs=in_specs, out_specs=out_specs, check_vma=False
    )
```

time: 381 us -> 105 us (0.28)
  waiting for transfers between devices: 259 us -> 0 us
  Pallas kernels: 0 us -> 96.7 us
  matrix products: 37.6 us -> 0 us
  local copies, waits for them, and re-layouts: 33.7 us -> 7.62 us
  starting transfers between devices: 21.9 us -> 0 us
  other arithmetic: 13.8 us -> 0.02 us
  between operations: 14.3 us -> 0.66 us
    unnamed x4 -> x0, waiting for transfers between devices: 150 us -> none
    all_gather x2 -> x0, waiting for transfers between devices: 109 us -> none  [fetch_forward(): return lax.all_gather(shard, 'seq', axis=0, tiled=True)]
    pallas_call x0 -> x1, Pallas kernels: none -> 96.7 us  [per_device(): pl.pallas_call(kernel, out_shape=(jax.ShapeDtypeStruct((L, C), BF), jax.S...]
    dot_general x18 -> x0, matrix products: 37.6 us -> none  [the longest x6 15.1 us: forward_layer(): jnp.dot(padded[tap * spacing:tap * spacing + length], weight[:, tap, :],...]
    slice x6 -> x0, local copies, waits for them, and re-layouts: 24.6 us -> none  [the longest x2 23.7 us: forward_layer(): weight[:, tap, :]]
    ppermute x8 -> x0, starting transfers between devices: 21.8 us -> none  [the longest x4 12 us: padded_2(): lax.ppermute(lax.slice_in_dim(block, block.shape[dim] - width, None, axis...]
    mul x2 -> x0, other arithmetic: 6.5 us -> none  [weight_term(): return jnp.stack(terms, axis=1) * grad_scale]
    convert_element_type x3 -> x0, other arithmetic: 5.34 us -> none  [the longest x2 4.12 us: backward_layer(): return passed.astype(jnp.bfloat16)]
  transfers between devices with their start and end apart: 11 -> 0, of which waited for: 3 -> 0; matrix products, arithmetic and copies ran while one was open for 17% -> 0% of each run, Pallas kernels for 0% -> 0%
where the time goes in v1:
time: 105 us
  Pallas kernels  96.7 us (92%)
  local copies, waits for them, and re-layouts  7.62 us (7%)
    pallas_call x1, Pallas kernels, per_device(): pl.pallas_call(kernel, out_shape=(jax.ShapeDtypeStruct((L, C), BF), jax.S...  96.7 us
    unnamed x6, local copies, waits for them, and re-layouts  5.24 us

profile of v1, /device:TPU:1, one launch (start us, length us, event | category | flops | bytes accessed | tf_op | source)
XLA Modules:
  0.0 105.0 jit_solution(1367374143794010824)
XLA Ops:
  0.6 0.8 copy_bitcast_fusion
  1.5 0.6 pad.4.refs_2_
  2.1 96.7 %shard_map.75 = (bf16[1024,768]{1,0:T(8,128)(2,1)}, bf16[1024,768]{1,0:T(8,128)(2,1)}, f32[2,3,8,768]{3,2,1,0:T(8,128)}) custom-call(bf16[1024,768]{1,0:T(8,128)(2,1)} %refs_0_.1, bf16[1024,768]{1,0:T(8,128)(2,1)} %refs_1_.1, bf16[2,3,8,768]{3,2,1,0:T(8,128)(2,1)} %pad.4.refs_2_), custom_call_target="tpu_custom_call" | custom-call | tf_op jit(solution)/shard_map/pallas_call | solution.py:438
  98.8 0.9 slice_bitcast_fusion
  99.8 0.7 copy.11
  100.4 0.7 copy.10
  101.1 0.0 copy-start
  101.1 2.8 %copy.16 = bf16[1024,768]{1,0:T(8,128)(2,1)} copy(bf16[1024,768]{1,0:T(8,128)(2,1)} %get-tuple-element.22) | data formatting | bytes 3145728
  103.9 0.0 copy-done
  103.9 1.1 %copy.17 = bf16[1024,768]{1,0:T(8,128)(2,1)} copy(bf16[1024,768]{1,0:T(8,128)(2,1)S(1)} %copy-done) | data formatting | bytes 3145728
  (2 shorter events, 0.0 us)
Async XLA Ops:
  101.1 2.8 %copy-start = (bf16[1024,768]{1,0:T(8,128)(2,1)S(1)}, bf16[1024,768]{1,0:T(8,128)(2,1)}, u32[]{:S(2)}) copy-start(bf16[1024,768]{1,0:T(8,128)(2,1)} %get-tuple-element.23) | copy-start | bytes 4718596

commit v2 on v1

v2 whole, which is shorter than its diff:
```python
import math

import jax
import jax.numpy as jnp
from jax import lax
from jax.experimental import pallas as pl
from jax.experimental.pallas import tpu as pltpu
from jax.sharding import PartitionSpec as P

DILATION_A = 32
DILATION_B = 64
N = 128
C = 768
HALF = C // 2
L = 1024
BF = jnp.bfloat16
F32 = jnp.float32
MESH = pl.DeviceIdType.MESH
TM = 256


def body(
    scale,
    x_hbm, g_hbm, w_hbm,
    out_hbm, ig_hbm, gr_hbm,
    xb, a1p, h, a2p, g2p, g1p, at1, at2, W, s1, s2, ir1, ir2, G, stage, R0, A, H1, R1, B, S2R, T, S3S, S3R, gout,
    lsem, cs, cr, hs, hr, p1s, p1r, p2s, p2r, fs, fr, bs, br,
    x0s, x0r, x1s, x1r, x2s, x2r, x3s, x3r, x4s, x4r,
):
    me = lax.axis_index("seq")
    c = lax.rem(me, 2)
    z = lax.rem(me // 2, 4)
    y = lax.rem(me // 8, 4)
    x = me // 32

    def place(df, ds, o):
        dx, dy = (df, ds) if o == 0 else (ds, df)
        return lax.rem(x + dx, 4), lax.rem(y + dy, 4)

    def dev(df, ds, o):
        xx, yy = place(df, ds, o)
        return (4 * xx + yy) * 8 + 2 * z + c

    firsts = (x, y)
    seconds = (y, x)
    sibling = me + 1 - 2 * c
    left = lax.rem(me + N - 1, N)
    right = lax.rem(me + 1, N)
    column = (4 * x + y) * 8

    def remote(src, dst, send, recv, target):
        return pltpu.make_async_remote_copy(
            src_ref=src, dst_ref=dst, send_sem=send, recv_sem=recv, device_id=(target,), device_id_type=MESH
        )

    sent = []

    def send(*args):
        copy = remote(*args)
        copy.start()
        sent.append(copy)

    def arrived(dst, send_sem, recv_sem):
        remote(dst, dst, send_sem, recv_sem, sibling).wait_recv()

    load_x = pltpu.make_async_copy(x_hbm, xb, lsem.at[0])
    load_x.start()
    load_g = pltpu.make_async_copy(g_hbm, g2p.at[pl.ds(DILATION_B, L)], lsem.at[1])
    load_g.start()

    barrier = pltpu.get_barrier_semaphore()
    greet = [column + lax.rem(me - column + k, 8) for k in range(1, 8)]
    for o in range(2):
        greet += [dev(k, 0, o) for k in range(1, 4)]
    greet += [left, right]
    for target in greet:
        pl.semaphore_signal(barrier, inc=1, device_id=(target,), device_id_type=MESH)

    cc = z // 2
    slot = 2 * lax.rem(z, 2) + c

    def column_send(l):
        for zt in range(4):
            target = column + 2 * zt + cc

            @pl.when(target != me)
            def _():
                remote(w_hbm.at[l], stage.at[l, :, slot], cs.at[l, zt], cr.at[l, slot], target).start()

            @pl.when(target == me)
            def _():
                pltpu.make_async_copy(w_hbm.at[l], stage.at[l, :, slot], cr.at[l, slot]).start()

    def column_wait(l):
        for j in range(4):
            source = column + 4 * c + j

            @pl.when(source != me)
            def _():
                arrived(stage.at[l, :, j], cs.at[l, 0], cr.at[l, j])

            @pl.when(source == me)
            def _():
                pltpu.make_async_copy(w_hbm.at[l], stage.at[l, :, j], cr.at[l, j]).wait()

    def column_sent(l):
        for zt in range(4):
            target = column + 2 * zt + cc

            @pl.when(target != me)
            def _():
                remote(w_hbm.at[l], stage.at[l, :, slot], cs.at[l, zt], cr.at[l, slot], target).wait_send()

    def repack(l):
        row = lax.broadcasted_iota(jnp.int32, (24, 32), 0)
        col = lax.broadcasted_iota(jnp.int32, (24, 32), 1)
        pick = jnp.where(col == (row // 6) * 8 + lax.rem(row, 6), 1.0, 0.0).astype(BF)
        for k in range(3):
            dense = jnp.dot(pick, stage[l, k].reshape(32, C), preferred_element_type=F32)
            W[l, k, x, y, c] = dense.astype(BF)

    OFFSET = (0, 3, 1, 2)

    def share(k, o, d):
        width = 128 if (k + o + d) % 2 == 0 else 256
        return HALF * o + (0 if d == 0 else HALF - width), width

    def grp(l, k, o, n, half, start=None, width=HALF):
        cols = pl.ds(HALF * o if start is None else start, width)
        s = lax.rem(seconds[o] + OFFSET[n], 4)
        if o == 0:
            return W.at[l, k, :, s, half, :, cols]
        return W.at[l, k, s, :, half, :, cols]

    def ag_p1(l, k):
        for o in range(2):
            for d in range(1, 4):
                ref = W.at[l, k, x, y, c, :, pl.ds(HALF * o, HALF)]
                send(ref, ref, p1s.at[l, k, o, d - 1], p1r.at[l, k, o, d - 1], dev(d, 0, o))

    def to_sibling(l, k, o, n):
        ref = grp(l, k, o, n, c)
        send(ref, ref, bs.at[l, k, o, n], br.at[l, k, o, n], sibling)

    def ag_p2(l, k):
        for o in range(2):
            for d in range(1, 4):
                xx, yy = place(4 - d, 0, o)
                arrived(W.at[l, k, xx, yy, c, :, pl.ds(HALF * o, HALF)], p1s.at[l, k, o, d - 1], p1r.at[l, k, o, d - 1])
            for d in range(2):
                ref = grp(l, k, o, 0, c)
                send(ref, ref, p2s.at[l, k, o, d], p2r.at[l, k, o, d], dev(0, 1 + 2 * d, o))
            to_sibling(l, k, o, 0)

    def ag_f(l, k):
        for o in range(2):
            for d in range(2):
                arrived(grp(l, k, o, 1 + d, c), p2s.at[l, k, o, d], p2r.at[l, k, o, d])
                part = grp(l, k, o, 1 + d, c, *share(k, o, d))
                send(part, part, fs.at[l, k, o, d], fr.at[l, k, o, d], dev(0, 1 + 2 * d, o))
                to_sibling(l, k, o, 1 + d)

    def ag_e(l, k):
        for o in range(2):
            for d in range(2):
                arrived(grp(l, k, o, 3, c, *share(k, o, d)), fs.at[l, k, o, d], fr.at[l, k, o, d])
            to_sibling(l, k, o, 3)

    def ag_done(l, k):
        for o in range(2):
            for n in range(4):
                arrived(grp(l, k, o, n, 1 - c), bs.at[l, k, o, n], br.at[l, k, o, n])

    def halo_copies(ref, d, n):
        return (
            remote(ref.at[pl.ds(L, d)], ref.at[pl.ds(0, d)], hs.at[n, 0], hr.at[n, 0], right),
            remote(ref.at[pl.ds(d, d)], ref.at[pl.ds(L + d, d)], hs.at[n, 1], hr.at[n, 1], left),
        )

    def halo_send(ref, d, n):
        for copy in halo_copies(ref, d, n):
            copy.start()

    def halo_sent(ref, d, n):
        for copy in halo_copies(ref, d, n):
            copy.wait_send()

    def halo_wait(ref, d, n):
        arrived(ref.at[pl.ds(0, d)], hs.at[n, 0], hr.at[n, 0])
        arrived(ref.at[pl.ds(L + d, d)], hs.at[n, 1], hr.at[n, 1])

        @pl.when(me == 0)
        def _():
            ref[pl.ds(0, d), :] = jnp.zeros((d, C), BF)

        @pl.when(me == N - 1)
        def _():
            ref[pl.ds(L + d, d), :] = jnp.zeros((d, C), BF)

    def activate(xf, t0, ap, d, at, s_ref, ir_ref):
        inv = lax.rsqrt(jnp.mean(xf * xf, axis=-1, keepdims=True) + 1e-06)
        normed = xf * inv
        gate = 0.5 * (1.0 + lax.erf(normed * 0.7071067811865476))
        active = (normed * gate).astype(BF)
        ap[pl.ds(pl.multiple_of(t0 + d, 32), TM), :] = active
        at[:, pl.ds(t0, TM)] = active.T
        s_ref[pl.ds(t0, TM), :] = gate + normed * jnp.exp(-0.5 * normed * normed) * 0.3989422804014327
        ir_ref[pl.ds(t0, TM), :] = inv

    def tiles(fn, count, size=TM, low=0):
        def step(i, carry):
            fn(pl.multiple_of(i * size, size))
            return carry

        lax.fori_loop(low, count, step, 0)

    def tile(fn, i):
        tiles(fn, i + 1, TM, i)

    def weight(l, k):
        return W[l, k].reshape(C, C)

    def term(ap, d, l, k, t0):
        return jnp.dot(ap[pl.ds(pl.multiple_of(t0 + k * d, 32), TM), :], weight(l, k), preferred_element_type=F32)

    def forward(ap, d, l, t0):
        acc = jnp.zeros((TM, C), F32)
        for k in range(3):
            acc = acc + term(ap, d, l, k, t0)
        return acc

    def backward(gp, d, l, x_ref, s_ref, ir_ref, t0):
        acc = jnp.zeros((TM, C), F32)
        for k in range(3):
            acc = acc + lax.dot_general(
                gp[pl.ds(pl.multiple_of(t0 + (2 - k) * d, 32), TM), :],
                weight(l, k),
                (((1,), (1,)), ((), ())),
                preferred_element_type=F32,
            )
        rows = pl.ds(t0, TM)
        inv = ir_ref[rows, :]
        normed = x_ref[rows, :].astype(F32) * inv
        norm_grad = acc * s_ref[rows, :]
        mean = jnp.mean(norm_grad * normed, axis=-1, keepdims=True)
        own = gp[pl.ds(pl.multiple_of(t0 + d, 32), TM), :].astype(F32)
        return (own + inv * (norm_grad - normed * mean)).astype(BF)

    def weight_grad(at, gp, d, l, k):
        rhs_start = (2 - k) * d

        def one(t0):
            acc = jnp.dot(at[pl.ds(t0, 384), :], gp[pl.ds(rhs_start, L), :], preferred_element_type=F32)
            G[l, k, pl.ds(t0 // 48, 8)] = acc.astype(BF).reshape(8, 2, 24, C)

        tiles(one, 2, 384)
        send(G.at[l, k, :, 1 - c], R0.at[l, k], x0s.at[l, k], x0r.at[l, k], sibling)

    def act_one(t0):
        activate(xb[pl.ds(t0, TM), :].astype(F32), t0, a1p, DILATION_A, at1, s1, ir1)

    def first_a(t0):
        s2[pl.ds(t0, TM), :] = term(a1p, DILATION_A, 0, 1, t0)

    def first_b(t0):
        s2[pl.ds(t0, TM), :] += term(a1p, DILATION_A, 0, 0, t0)

    def first(t0):
        mixed = s2[pl.ds(t0, TM), :] + term(a1p, DILATION_A, 0, 2, t0)
        out = (xb[pl.ds(t0, TM), :].astype(F32) + mixed).astype(BF)
        h[pl.ds(t0, TM), :] = out
        activate(out.astype(F32), t0, a2p, DILATION_B, at2, s2, ir2)

    def second(t0):
        passed = backward(g2p, DILATION_B, 1, h, s2, ir2, t0)
        g1p[pl.ds(pl.multiple_of(t0 + DILATION_A, 32), TM), :] = passed

    def last_forward(t0):
        mixed = forward(a2p, DILATION_B, 1, t0)
        rows = pl.ds(t0, TM)
        g2p[rows, :] = (h[rows, :].astype(F32) + mixed).astype(BF)

    def last_backward(t0):
        a2p[pl.ds(t0, TM), :] = backward(g1p, DILATION_A, 0, xb, s1, ir1, t0)

    store_out = pltpu.make_async_copy(g2p.at[pl.ds(0, L)], out_hbm, lsem.at[4])
    store_in = pltpu.make_async_copy(a2p.at[pl.ds(0, L)], ig_hbm, lsem.at[5])

    def rs1(l, k):
        arrived(R0.at[l, k], x0s.at[l, k], x0r.at[l, k])

        def add(b, carry):
            hi = b // 4
            lo = lax.rem(b, 4)
            total = G[l, k, b, c] + R0[l, k, b]
            A[l, k, 0, lo, hi] = total[:, :HALF]
            A[l, k, 1, hi, lo] = total[:, HALF:]
            return carry

        lax.fori_loop(0, 16, add, 0)
        for o in range(2):
            far = lax.rem(seconds[o] + 2, 4)
            for d in range(2):
                start, width = share(k, o, d)
                cols = pl.ds(start - HALF * o, width)
                send(
                    A.at[l, k, o, far, :, :, cols], H1.at[l, k, o, :, :, cols],
                    x1s.at[l, k, o, d], x1r.at[l, k, o, d], dev(0, 1 + 2 * d, o),
                )

    def rs2(l, k):
        for o in range(2):
            for d in range(2):
                start, width = share(k, o, d)
                cols = pl.ds(start - HALF * o, width)
                arrived(H1.at[l, k, o, :, :, cols], x1s.at[l, k, o, d], x1r.at[l, k, o, d])
                near = lax.rem(seconds[o] + 1 + 2 * d, 4)
                A[l, k, o, near, :, :, cols] = A[l, k, o, near, :, :, cols] + H1[l, k, o, :, :, cols]
                send(
                    A.at[l, k, o, near], R1.at[l, k, o, d],
                    x2s.at[l, k, o, d], x2r.at[l, k, o, d], dev(0, 1 + 2 * d, o),
                )

    def rs3(l, k):
        for o in range(2):
            for d in range(2):
                arrived(R1.at[l, k, o, d], x2s.at[l, k, o, d], x2r.at[l, k, o, d])
            B[l, k, o] = (
                A[l, k, o, seconds[o]].astype(F32) + R1[l, k, o, 0].astype(F32) + R1[l, k, o, 1].astype(F32)
            ).astype(BF)
            for d in range(1, 4):
                send(
                    B.at[l, k, o, lax.rem(firsts[o] + d, 4)], S2R.at[l, k, o, d - 1],
                    x3s.at[l, k, o, d - 1], x3r.at[l, k, o, d - 1], dev(d, 0, o),
                )

    def rs4(l, k):
        for o in range(2):
            for d in range(1, 4):
                arrived(S2R.at[l, k, o, d - 1], x3s.at[l, k, o, d - 1], x3r.at[l, k, o, d - 1])
            total = B[l, k, o, firsts[o]].astype(F32)
            for d in range(3):
                total = total + S2R[l, k, o, d].astype(F32)
            T[pl.ds(0, 24), pl.ds(HALF * o, HALF)] = total
        T[pl.ds(24, 8), :] = jnp.zeros((8, C), F32)
        for j in range(4):
            S3S[l, j, k] = T[pl.ds(6 * j, 8), :].astype(BF)

    def rs5(l):
        for j in range(4):
            target = column + 4 * c + j

            @pl.when(target != me)
            def _():
                remote(S3S.at[l, j], S3R.at[l, z], x4s.at[l, j], x4r.at[l, z], target).start()

            @pl.when(target == me)
            def _():
                S3R[l, z] = S3S[l, j]

    def rs6(l):
        for zs in range(4):
            source = column + 2 * zs + cc

            @pl.when(source != me)
            def _():
                arrived(S3R.at[l, zs], x4s.at[l, 0], x4r.at[l, zs])

        total = S3R[l, 0].astype(F32)
        for zs in range(1, 4):
            total = total + S3R[l, zs].astype(F32)
        gout[l] = total * scale
        pltpu.make_async_copy(gout.at[l], gr_hbm.at[l], lsem.at[2 + l]).start()

    def rs_sent(l):
        for j in range(4):
            target = column + 4 * c + j

            @pl.when(target != me)
            def _():
                remote(S3S.at[l, j], S3R.at[l, z], x4s.at[l, j], x4r.at[l, z], target).wait_send()

    load_x.wait()
    tiles(act_one, 2)
    pl.semaphore_wait(barrier, len(greet))
    column_send(0)
    column_send(1)
    tiles(act_one, 4, TM, 2)
    column_wait(0)
    repack(0)
    ag_p1(0, 1)
    ag_p1(0, 0)
    ag_p1(0, 2)
    halo_send(a1p, DILATION_A, 0)
    column_wait(1)
    repack(1)
    ag_p2(0, 1)
    ag_p2(0, 0)
    ag_p2(0, 2)
    load_g.wait()
    ag_f(0, 1)
    ag_p1(1, 1)
    ag_p1(1, 0)
    ag_p1(1, 2)
    ag_f(0, 0)
    halo_send(g2p, DILATION_B, 2)
    halo_wait(a1p, DILATION_A, 0)
    ag_e(0, 1)
    ag_f(0, 2)
    ag_p2(1, 1)
    ag_done(0, 1)
    tiles(first_a, 4)
    ag_e(0, 0)
    ag_p2(1, 0)
    ag_p2(1, 2)
    ag_e(0, 2)
    ag_done(0, 0)
    tiles(first_b, 4)
    ag_done(0, 2)
    ag_f(1, 1)
    tiles(first, 2)
    ag_f(1, 0)
    ag_e(1, 1)
    tiles(first, 4, TM, 2)
    ag_f(1, 2)
    ag_e(1, 0)
    halo_send(a2p, DILATION_B, 1)
    halo_wait(g2p, DILATION_B, 2)
    weight_grad(at2, g2p, DILATION_B, 1, 1)
    weight_grad(at2, g2p, DILATION_B, 1, 2)
    ag_e(1, 2)
    rs1(1, 1)
    weight_grad(at2, g2p, DILATION_B, 1, 0)
    rs1(1, 2)
    for k in range(3):
        ag_done(1, k)
    tile(second, 0)
    rs2(1, 1)
    tile(second, 1)
    rs1(1, 0)
    rs2(1, 2)
    tile(second, 2)
    rs3(1, 1)
    tile(second, 3)
    halo_send(g1p, DILATION_A, 3)
    rs2(1, 0)
    rs3(1, 2)
    weight_grad(at1, g1p, DILATION_A, 0, 1)
    rs4(1, 1)
    halo_wait(g1p, DILATION_A, 3)
    weight_grad(at1, g1p, DILATION_A, 0, 2)
    rs1(0, 1)
    rs3(1, 0)
    weight_grad(at1, g1p, DILATION_A, 0, 0)
    rs1(0, 2)
    rs4(1, 2)
    halo_wait(a2p, DILATION_B, 1)
    halo_sent(g2p, DILATION_B, 2)
    tile(last_forward, 0)
    rs1(0, 0)
    rs2(0, 1)
    tile(last_forward, 1)
    rs4(1, 0)
    rs5(1)
    rs2(0, 2)
    tile(last_forward, 2)
    rs2(0, 0)
    rs3(0, 1)
    tile(last_forward, 3)
    store_out.start()
    rs3(0, 2)
    rs6(1)
    halo_sent(a2p, DILATION_B, 1)
    tile(last_backward, 0)
    rs3(0, 0)
    rs4(0, 1)
    tile(last_backward, 1)
    rs4(0, 2)
    tile(last_backward, 2)
    rs4(0, 0)
    rs5(0)
    tile(last_backward, 3)
    store_in.start()
    rs6(0)

    for copy in sent:
        copy.wait_send()
    halo_sent(a1p, DILATION_A, 0)
    halo_sent(g1p, DILATION_A, 3)
    for l in range(2):
        column_sent(l)
        rs_sent(l)
        pltpu.make_async_copy(gout.at[l], gr_hbm.at[l], lsem.at[2 + l]).wait()
    store_out.wait()
    store_in.wait()


def per_device(inputs, weight_one, weight_two, cotangent):
    scale = 1.0 / math.sqrt(inputs.shape[0] * lax.axis_size("seq"))
    shards = jnp.stack([weight_one, weight_two]).transpose(0, 2, 1, 3)
    shards = jnp.pad(shards, ((0, 0), (0, 0), (0, 2), (0, 0)))
    anywhere = pl.BlockSpec(memory_space=pl.ANY)
    vmem = pltpu.VMEM
    dma = pltpu.SemaphoreType.DMA

    def kernel(*refs):
        body(scale, *refs)

    outputs, input_grad, grads = pl.pallas_call(
        kernel,
        out_shape=(
            jax.ShapeDtypeStruct((L, C), BF),
            jax.ShapeDtypeStruct((L, C), BF),
            jax.ShapeDtypeStruct((2, 3, 8, C), F32),
        ),
        in_specs=[anywhere] * 3,
        out_specs=(anywhere,) * 3,
        scratch_shapes=[
            vmem((L, C), BF),
            vmem((L + 2 * DILATION_A, C), BF),
            vmem((L, C), BF),
            vmem((L + 2 * DILATION_B, C), BF),
            vmem((L + 2 * DILATION_B, C), BF),
            vmem((L + 2 * DILATION_A, C), BF),
            vmem((C, L), BF),
            vmem((C, L), BF),
            vmem((2, 3, 4, 4, 2, 24, C), BF),
            vmem((L, C), F32),
            vmem((L, C), F32),
            vmem((L, 1), F32),
            vmem((L, 1), F32),
            vmem((2, 3, 16, 2, 24, C), BF),
            vmem((2, 3, 4, 8, C), BF),
            vmem((2, 3, 16, 24, C), BF),
            vmem((2, 3, 2, 4, 4, 24, HALF), BF),
            vmem((2, 3, 2, 4, 24, HALF), BF),
            vmem((2, 3, 2, 2, 4, 24, HALF), BF),
            vmem((2, 3, 2, 4, 24, HALF), BF),
            vmem((2, 3, 2, 3, 24, HALF), BF),
            vmem((32, C), F32),
            vmem((2, 4, 3, 8, C), BF),
            vmem((2, 4, 3, 8, C), BF),
            vmem((2, 3, 8, C), F32),
            dma((6,)),
            dma((2, 4)), dma((2, 4)),
            dma((4, 2)), dma((4, 2)),
            dma((2, 3, 2, 3)), dma((2, 3, 2, 3)),
            dma((2, 3, 2, 2)), dma((2, 3, 2, 2)),
            dma((2, 3, 2, 2)), dma((2, 3, 2, 2)),
            dma((2, 3, 2, 4)), dma((2, 3, 2, 4)),
            dma((2, 3)), dma((2, 3)),
            dma((2, 3, 2, 2)), dma((2, 3, 2, 2)),
            dma((2, 3, 2, 2)), dma((2, 3, 2, 2)),
            dma((2, 3, 2, 3)), dma((2, 3, 2, 3)),
            dma((2, 4)), dma((2, 4)),
        ],
        compiler_params=pltpu.CompilerParams(
            collective_id=0, has_side_effects=True, vmem_limit_bytes=50500000
        ),
    )(inputs, cotangent, shards)
    grads = grads[:, :, :6, :].transpose(0, 2, 1, 3)
    return (outputs, input_grad, grads[0], grads[1])


def solution(mesh):
    in_specs = (P("seq", None), P("seq", None, None), P("seq", None, None), P("seq", None))
    out_specs = (P("seq", None), P("seq", None), P("seq", None, None), P("seq", None, None))
    return jax.shard_map(
        per_device, mesh=mesh, in_specs=in_specs, out_specs=out_specs, check_vma=False
    )
```

time: 105 us -> 93.6 us (0.89)
  Pallas kernels: 96.7 us -> 86.9 us
  local copies, waits for them, and re-layouts: 7.62 us -> 5.85 us
    pallas_call x1, Pallas kernels: 96.7 us -> 86.9 us  [per_device(): pl.pallas_call(kernel, out_shape=(jax.ShapeDtypeStruct((L, C), BF), jax.S...]
where the time goes in v2:
time: 93.6 us; the launch traced here: 93.4 us
  Pallas kernels  86.9 us (93%)
  local copies, waits for them, and re-layouts  5.85 us (6%)
    pallas_call x1, Pallas kernels, per_device(): pl.pallas_call(kernel, out_shape=(jax.ShapeDtypeStruct((L, C), BF), jax.S...  86.9 us
    unnamed x6, local copies, waits for them, and re-layouts  5.01 us

profile of v2, /device:TPU:1, one launch (start us, length us, event | category | flops | bytes accessed | tf_op | source)
XLA Modules:
  0.0 93.4 jit_solution(6259496103758235405)
XLA Ops:
  0.6 0.8 copy_bitcast_fusion
  1.5 0.0 copy-start
  1.5 1.4 %copy-done = bf16[1024,768]{1,0:T(8,128)(2,1)S(1)} copy-done((bf16[1024,768]{1,0:T(8,128)(2,1)S(1)}, bf16[1024,768]{1,0:T(8,128)(2,1)}, u32[]{:S(2)}) %copy-start) | copy-done | bytes 1572888
  2.9 86.9 %shard_map.75 = (bf16[1024,768]{1,0:T(8,128)(2,1)S(1)}, bf16[1024,768]{1,0:T(8,128)(2,1)S(1)}, f32[2,3,8,768]{3,2,1,0:T(8,128)S(1)}) custom-call(bf16[1024,768]{1,0:T(8,128)(2,1)S(1)} %copy-done, bf16[1024,768]{1,0:T(8,128)(2,1)} %refs_1_.1, bf16[2,3,8,768]{3,2,1,0:T(8,128)(2,1)S(1)} %pad.4.refs_2_), custom_call_target="tpu_custom_call" | custom-call | tf_op jit(solution)/shard_map/pallas_call | solution.py:509
  89.8 0.7 copy.11
  90.5 0.7 copy.10
  91.1 1.1 %copy.16 = bf16[1024,768]{1,0:T(8,128)(2,1)} copy(bf16[1024,768]{1,0:T(8,128)(2,1)S(1)} %get-tuple-element.22) | data formatting | bytes 3145728
  92.3 1.1 %copy.17 = bf16[1024,768]{1,0:T(8,128)(2,1)} copy(bf16[1024,768]{1,0:T(8,128)(2,1)S(1)} %get-tuple-element.23) | data formatting | bytes 3145728
  (4 shorter events, 0.1 us)
Async XLA Ops:
  1.5 1.4 %copy-start = (bf16[1024,768]{1,0:T(8,128)(2,1)S(1)}, bf16[1024,768]{1,0:T(8,128)(2,1)}, u32[]{:S(2)}) copy-start(bf16[1024,768]{1,0:T(8,128)(2,1)} %refs_0_.1) | copy-start | bytes 4718596

commit v3 on v2

--- a/solution.py
+++ b/solution.py
@@ -436,13 +436,13 @@
         ag_done(1, k)
     tile(second, 0)
     rs2(1, 1)
-    tile(second, 1)
+    tile(second, 3)
+    halo_send(g1p, DILATION_A, 3)
     rs1(1, 0)
     rs2(1, 2)
+    tile(second, 1)
+    rs3(1, 1)
     tile(second, 2)
-    rs3(1, 1)
-    tile(second, 3)
-    halo_send(g1p, DILATION_A, 3)
     rs2(1, 0)
     rs3(1, 2)
     weight_grad(at1, g1p, DILATION_A, 0, 1)

time: 93.6 us -> 92.4 us (0.987)
  Pallas kernels: 86.9 us -> 85.6 us
    pallas_call x1, Pallas kernels: 86.9 us -> 85.6 us  [per_device(): pl.pallas_call(kernel, out_shape=(jax.ShapeDtypeStruct((L, C), BF), jax.S...]
where the time goes in v3:
time: 92.4 us; the launch traced here: 92.2 us
  Pallas kernels  85.6 us (93%)
  local copies, waits for them, and re-layouts  5.85 us (6%)
    pallas_call x1, Pallas kernels, per_device(): pl.pallas_call(kernel, out_shape=(jax.ShapeDtypeStruct((L, C), BF), jax.S...  85.6 us
    unnamed x6, local copies, waits for them, and re-layouts  5.01 us

profile of v3, /device:TPU:1, one launch (start us, length us, event | category | flops | bytes accessed | tf_op | source)
XLA Modules:
  0.0 92.2 jit_solution(18195376249762557657)
XLA Ops:
  0.6 0.8 copy_bitcast_fusion
  1.5 0.0 copy-start
  1.5 1.4 %copy-done = bf16[1024,768]{1,0:T(8,128)(2,1)S(1)} copy-done((bf16[1024,768]{1,0:T(8,128)(2,1)S(1)}, bf16[1024,768]{1,0:T(8,128)(2,1)}, u32[]{:S(2)}) %copy-start) | copy-done | bytes 1572888
  2.9 85.6 %shard_map.75 = (bf16[1024,768]{1,0:T(8,128)(2,1)S(1)}, bf16[1024,768]{1,0:T(8,128)(2,1)S(1)}, f32[2,3,8,768]{3,2,1,0:T(8,128)S(1)}) custom-call(bf16[1024,768]{1,0:T(8,128)(2,1)S(1)} %copy-done, bf16[1024,768]{1,0:T(8,128)(2,1)} %refs_1_.1, bf16[2,3,8,768]{3,2,1,0:T(8,128)(2,1)S(1)} %pad.4.refs_2_), custom_call_target="tpu_custom_call" | custom-call | tf_op jit(solution)/shard_map/pallas_call | solution.py:509
  88.5 0.7 copy.11
  89.2 0.7 copy.10
  89.9 1.1 %copy.16 = bf16[1024,768]{1,0:T(8,128)(2,1)} copy(bf16[1024,768]{1,0:T(8,128)(2,1)S(1)} %get-tuple-element.22) | data formatting | bytes 3145728
  91.0 1.1 %copy.17 = bf16[1024,768]{1,0:T(8,128)(2,1)} copy(bf16[1024,768]{1,0:T(8,128)(2,1)S(1)} %get-tuple-element.23) | data formatting | bytes 3145728
  (4 shorter events, 0.1 us)
Async XLA Ops:
  1.5 1.4 %copy-start = (bf16[1024,768]{1,0:T(8,128)(2,1)S(1)}, bf16[1024,768]{1,0:T(8,128)(2,1)}, u32[]{:S(2)}) copy-start(bf16[1024,768]{1,0:T(8,128)(2,1)} %refs_0_.1) | copy-start | bytes 4718596

commit v4 on v3

--- a/solution.py
+++ b/solution.py
@@ -289,15 +289,14 @@
     def rs1(l, k):
         arrived(R0.at[l, k], x0s.at[l, k], x0r.at[l, k])
 
-        def add(b, carry):
-            hi = b // 4
-            lo = lax.rem(b, 4)
-            total = G[l, k, b, c] + R0[l, k, b]
-            A[l, k, 0, lo, hi] = total[:, :HALF]
-            A[l, k, 1, hi, lo] = total[:, HALF:]
+        def add(hi, carry):
+            for lo in range(4):
+                total = G[l, k, 4 * hi + lo, c] + R0[l, k, 4 * hi + lo]
+                A[l, k, 0, lo, hi] = total[:, :HALF]
+                A[l, k, 1, hi, lo] = total[:, HALF:]
             return carry
 
-        lax.fori_loop(0, 16, add, 0)
+        lax.fori_loop(0, 4, add, 0)
         for o in range(2):
             far = lax.rem(seconds[o] + 2, 4)
             for d in range(2):
@@ -384,19 +383,19 @@
     tiles(act_one, 2)
     pl.semaphore_wait(barrier, len(greet))
     column_send(0)
-    column_send(1)
     tiles(act_one, 4, TM, 2)
     column_wait(0)
     repack(0)
     ag_p1(0, 1)
     ag_p1(0, 0)
     ag_p1(0, 2)
+    column_send(1)
     halo_send(a1p, DILATION_A, 0)
-    column_wait(1)
-    repack(1)
     ag_p2(0, 1)
     ag_p2(0, 0)
     ag_p2(0, 2)
+    column_wait(1)
+    repack(1)
     load_g.wait()
     ag_f(0, 1)
     ag_p1(1, 1)
@@ -460,16 +459,15 @@
     rs1(0, 0)
     rs2(0, 1)
     tile(last_forward, 1)
+    rs2(0, 2)
     rs4(1, 0)
     rs5(1)
-    rs2(0, 2)
     tile(last_forward, 2)
     rs2(0, 0)
     rs3(0, 1)
     tile(last_forward, 3)
     store_out.start()
     rs3(0, 2)
-    rs6(1)
     halo_sent(a2p, DILATION_B, 1)
     tile(last_backward, 0)
     rs3(0, 0)
@@ -481,6 +479,7 @@
     rs5(0)
     tile(last_backward, 3)
     store_in.start()
+    rs6(1)
     rs6(0)
 
     for copy in sent:

time: 92.4 us -> 91.7 us (level)
  no operation moved by 1% of the time
where the time goes in v4:
time: 91.7 us; the launch traced here: 91.5 us
  Pallas kernels  84.9 us (93%)
  local copies, waits for them, and re-layouts  5.85 us (6%)
    pallas_call x1, Pallas kernels, per_device(): pl.pallas_call(kernel, out_shape=(jax.ShapeDtypeStruct((L, C), BF), jax.S...  84.9 us
    unnamed x6, local copies, waits for them, and re-layouts  5.01 us

profile of v4, /device:TPU:1, one launch (start us, length us, event | category | flops | bytes accessed | tf_op | source)
XLA Modules:
  0.0 91.5 jit_solution(17334104194412209406)
XLA Ops:
  0.6 0.8 copy_bitcast_fusion
  1.5 0.0 copy-start
  1.5 1.4 %copy-done = bf16[1024,768]{1,0:T(8,128)(2,1)S(1)} copy-done((bf16[1024,768]{1,0:T(8,128)(2,1)S(1)}, bf16[1024,768]{1,0:T(8,128)(2,1)}, u32[]{:S(2)}) %copy-start) | copy-done | bytes 1572888
  2.9 84.9 %shard_map.75 = (bf16[1024,768]{1,0:T(8,128)(2,1)S(1)}, bf16[1024,768]{1,0:T(8,128)(2,1)S(1)}, f32[2,3,8,768]{3,2,1,0:T(8,128)S(1)}) custom-call(bf16[1024,768]{1,0:T(8,128)(2,1)S(1)} %copy-done, bf16[1024,768]{1,0:T(8,128)(2,1)} %refs_1_.1, bf16[2,3,8,768]{3,2,1,0:T(8,128)(2,1)S(1)} %pad.4.refs_2_), custom_call_target="tpu_custom_call" | custom-call | tf_op jit(solution)/shard_map/pallas_call | solution.py:508
  87.9 0.7 copy.11
  88.5 0.7 copy.10
  89.2 1.1 %copy.16 = bf16[1024,768]{1,0:T(8,128)(2,1)} copy(bf16[1024,768]{1,0:T(8,128)(2,1)S(1)} %get-tuple-element.22) | data formatting | bytes 3145728
  90.4 1.1 %copy.17 = bf16[1024,768]{1,0:T(8,128)(2,1)} copy(bf16[1024,768]{1,0:T(8,128)(2,1)S(1)} %get-tuple-element.23) | data formatting | bytes 3145728
  (4 shorter events, 0.1 us)
Async XLA Ops:
  1.5 1.4 %copy-start = (bf16[1024,768]{1,0:T(8,128)(2,1)S(1)}, bf16[1024,768]{1,0:T(8,128)(2,1)}, u32[]{:S(2)}) copy-start(bf16[1024,768]{1,0:T(8,128)(2,1)} %refs_0_.1) | copy-start | bytes 4718596

commit v5 on v4

--- a/solution.py
+++ b/solution.py
@@ -289,14 +289,15 @@
     def rs1(l, k):
         arrived(R0.at[l, k], x0s.at[l, k], x0r.at[l, k])
 
-        def add(hi, carry):
-            for lo in range(4):
+        def add(pair, carry):
+            for n in range(8):
+                hi, lo = 2 * pair + n // 4, n % 4
                 total = G[l, k, 4 * hi + lo, c] + R0[l, k, 4 * hi + lo]
                 A[l, k, 0, lo, hi] = total[:, :HALF]
                 A[l, k, 1, hi, lo] = total[:, HALF:]
             return carry
 
-        lax.fori_loop(0, 4, add, 0)
+        lax.fori_loop(0, 2, add, 0)
         for o in range(2):
             far = lax.rem(seconds[o] + 2, 4)
             for d in range(2):

time: 91.7 us -> 91.8 us (level)
  no operation moved by 1% of the time
where the time goes in v5:
time: 91.8 us; the launch traced here: 91.6 us
  Pallas kernels  85 us (93%)
  local copies, waits for them, and re-layouts  5.85 us (6%)
    pallas_call x1, Pallas kernels, per_device(): pl.pallas_call(kernel, out_shape=(jax.ShapeDtypeStruct((L, C), BF), jax.S...  85 us
    unnamed x6, local copies, waits for them, and re-layouts  5.01 us

profile of v5, /device:TPU:1, one launch (start us, length us, event | category | flops | bytes accessed | tf_op | source)
XLA Modules:
  0.0 91.6 jit_solution(9665971769984687008)
XLA Ops:
  0.6 0.8 copy_bitcast_fusion
  1.5 0.0 copy-start
  1.5 1.4 %copy-done = bf16[1024,768]{1,0:T(8,128)(2,1)S(1)} copy-done((bf16[1024,768]{1,0:T(8,128)(2,1)S(1)}, bf16[1024,768]{1,0:T(8,128)(2,1)}, u32[]{:S(2)}) %copy-start) | copy-done | bytes 1572888
  2.9 85.0 %shard_map.75 = (bf16[1024,768]{1,0:T(8,128)(2,1)S(1)}, bf16[1024,768]{1,0:T(8,128)(2,1)S(1)}, f32[2,3,8,768]{3,2,1,0:T(8,128)S(1)}) custom-call(bf16[1024,768]{1,0:T(8,128)(2,1)S(1)} %copy-done, bf16[1024,768]{1,0:T(8,128)(2,1)} %refs_1_.1, bf16[2,3,8,768]{3,2,1,0:T(8,128)(2,1)S(1)} %pad.4.refs_2_), custom_call_target="tpu_custom_call" | custom-call | tf_op jit(solution)/shard_map/pallas_call | solution.py:509
  87.9 0.7 copy.11
  88.6 0.7 copy.10
  89.3 1.1 %copy.16 = bf16[1024,768]{1,0:T(8,128)(2,1)} copy(bf16[1024,768]{1,0:T(8,128)(2,1)S(1)} %get-tuple-element.22) | data formatting | bytes 3145728
  90.4 1.1 %copy.17 = bf16[1024,768]{1,0:T(8,128)(2,1)} copy(bf16[1024,768]{1,0:T(8,128)(2,1)S(1)} %get-tuple-element.23) | data formatting | bytes 3145728
  (4 shorter events, 0.1 us)
Async XLA Ops:
  1.5 1.4 %copy-start = (bf16[1024,768]{1,0:T(8,128)(2,1)S(1)}, bf16[1024,768]{1,0:T(8,128)(2,1)}, u32[]{:S(2)}) copy-start(bf16[1024,768]{1,0:T(8,128)(2,1)} %refs_0_.1) | copy-start | bytes 4718596
